TPU v7x, 256 devices: a whole 4x4x8 slice. The times are simulated.
256 devices in a mesh: ctx: 32 (over z, y_hi, core), head: 8 (over x, y_lo).
Axes of the slice: x: 4, y: 4 (y_hi: 2, y_lo: 2; y = y_hi * 2 + y_lo), z: 8, core: 2. Of those that a mesh axis runs over, the one named last changes fastest.
Arguments:
- queries: bfloat16 [20480, 2048], P('ctx', 'head'), may hold values from -8 to 8
- keys: bfloat16 [20480, 2048], P('ctx', 'head'), may hold values from -6 to 6
- values: bfloat16 [20480, 2048], P('ctx', 'head'), may hold values from -6 to 6
- key_weight: bfloat16 [16, 16, 128], P('head'), may hold values from -1.5 to 1.5
- value_weight: bfloat16 [16, 16, 128], P('head'), may hold values from -1.5 to 1.5
Outputs:
- attended: bfloat16 [20480, 2048], P(('ctx', 'head'))
All inputs are finite; a program needn't handle non-finite values.
Results may differ from a plain program's by a relative error of at most 0.0061.
Values may be sent and summed in bfloat16 or wider, within the bound.
No kernel may reach another device: no remote copies, remote signals or barrier semaphores. Data moves between devices by JAX's collectives and lax.ppermute only.
A program may use at most 64 MiB of HBM per device.

v0:
```python
import math

import jax
import jax.numpy as jnp
from jax import lax
from jax.sharding import PartitionSpec as P

query_span = 512
key_span = 1024


def from_partner(shard, axis, stride):
    return lax.ppermute(shard, axis, [(i, i ^ 1 << stride) for i in range(lax.axis_size(axis))])


def fold_rows(values_in, weight):
    row_count, channels = values_in.shape
    head_count, group_size, head_width = weight.shape
    grouped = values_in.reshape(row_count // group_size, group_size, head_count, head_width)
    folded = jnp.einsum("gjhd,hjd->ghd", grouped, weight, preferred_element_type=jnp.float32)
    return folded.astype(jnp.bfloat16).reshape(row_count // group_size, channels)


def attend(carried, query_heads, key_rows, value_rows):
    top_now, total_now, summed = carried
    query_count, head_count, head_width = query_heads.shape
    key_count = key_rows.shape[0]
    key_heads = key_rows.reshape(key_count, head_count, head_width)
    value_heads = value_rows.reshape(key_count, head_count, head_width)
    score_scale = 1.0 / math.sqrt(head_width)
    top_parts, total_parts, sum_parts = ([], [], [])
    for query_start in range(0, query_count, query_span):
        query_end = min(query_count, query_start + query_span)
        run_top = top_now[:, query_start:query_end]
        run_total = total_now[:, query_start:query_end]
        run_sum = summed[:, query_start:query_end]
        for key_start in range(0, key_count, key_span):
            key_end = min(key_count, key_start + key_span)
            scores = (
                jnp.einsum(
                    "qhd,khd->hqk",
                    query_heads[query_start:query_end],
                    key_heads[key_start:key_end],
                    preferred_element_type=jnp.float32,
                )
                * score_scale
            )
            new_top = jnp.maximum(run_top, jnp.max(scores, axis=2))
            factor = jnp.exp(run_top - new_top)
            weights = jnp.exp(scores - new_top[:, :, None])
            run_total = run_total * factor + jnp.sum(weights, axis=2)
            run_sum = run_sum * factor[:, :, None] + jnp.einsum(
                "hqk,khd->hqd",
                weights.astype(jnp.bfloat16),
                value_heads[key_start:key_end],
                preferred_element_type=jnp.float32,
            )
            run_top = new_top
        top_parts.append(run_top)
        total_parts.append(run_total)
        sum_parts.append(run_sum)
    return (
        jnp.concatenate(top_parts, 1),
        jnp.concatenate(total_parts, 1),
        jnp.concatenate(sum_parts, 1),
    )


def body(queries, keys, values, key_weight, value_weight):
    block_rows, channels = queries.shape
    head_count, group_size, head_width = key_weight.shape
    query_heads = queries.reshape(block_rows, head_count, head_width)
    folded_keys = fold_rows(keys, key_weight)
    folded_values = fold_rows(values, value_weight)
    carried = (
        jnp.full((head_count, block_rows), -jnp.inf, jnp.float32),
        jnp.zeros((head_count, block_rows), jnp.float32),
        jnp.zeros((head_count, block_rows, head_width), jnp.float32),
    )
    carried = attend(carried, query_heads, keys, values)
    bit_count = lax.axis_size("ctx").bit_length() - 1
    for bit_index in range(bit_count):
        far_keys, far_values = from_partner((keys, values), "ctx", bit_index)
        carried = attend(carried, query_heads, far_keys, far_values)
    carried = attend(
        carried,
        query_heads,
        lax.all_gather(folded_keys, "ctx", axis=0, tiled=True),
        lax.all_gather(folded_values, "ctx", axis=0, tiled=True),
    )
    top_now, total_now, summed = carried
    result = (summed / total_now[:, :, None]).astype(jnp.bfloat16)
    result = jnp.transpose(result, (1, 0, 2)).reshape(block_rows, head_count * head_width)
    return lax.all_to_all(result, "head", split_axis=0, concat_axis=1, tiled=True)


def solution(mesh):
    in_specs = (
        P("ctx", "head"),
        P("ctx", "head"),
        P("ctx", "head"),
        P("head", None, None),
        P("head", None, None),
    )
    out_specs = P(("ctx", "head"), None)
    return jax.shard_map(body, mesh=mesh, in_specs=in_specs, out_specs=out_specs, check_vma=False)
```

profile of v0, /device:TPU:16, one launch (start us, length us, event | category | flops | bytes accessed | tf_op | source)
XLA Modules:
  0.0 195.2 jit_solution(15290584683478375523)
XLA Ops:
  0.0 1.9 copy.149
  1.9 7.2 %collective-permute-start.8 = (bf16[640,256]{0,1:T(8,128)(2,1)}, bf16[640,256]{0,1:T(8,128)(2,1)}, u32[]{:S(2)}, u32[]{:S(2)}) collective-permute-start(bf16[640,256]{0,1:T(8,128)(2,1)} %copy.149), channel_id=1, source_target_pairs={{0,128},{8,136},{16,144},{24,152},{32,160},{40,168},{48,176},{56,1... | collective-permute-start | bytes 983048 | tf_op jit(solution)/shard_map/ppermute | solution.py:13
  9.1 1.5 collective-permute-start.6
  10.6 1.0 collective-permute-start.4
  11.6 0.3 collective-permute-start.2
  11.9 1.1 reshape.407
  13.0 0.7 bitcast_convert_fusion.1
  13.7 0.4 multiply_reduce_fusion.7
  14.1 56.2 %all_gather.6 = bf16[1280,256]{1,0:T(8,128)(2,1)S(1)} all-gather(bf16[40,256]{1,0:T(8,128)(2,1)S(1)} %bitcast.164), channel_id=1, replica_groups=mesh['ctx'=32,'head'=8] {'ctx'}, dimensions={0}, use_global_device_ids=true | all-gather | bytes 675840 | tf_op jit(solution)/shard_map/all_gather | solution.py:88
  70.3 0.8 copy-done.4
  71.6 0.4 fusion.173
  72.0 0.9 fusion.168
  73.0 2.7 %bitcast_reduce_fusion = (f32[2,512]{1,0:T(2,128)S(1)}, f32[2,1024,512]{2,1,0:T(8,128)}) fusion(bf16[1024,2,128]{0,2,1:T(8,128)(2,1)S(1)} %bitcast.146, bf16[512,2,128]{0,2,1:T(8,128)(2,1)S(1)} %bitcast.127), kind=kOutput, calls=%fused_computation.1 | convolution fusion | flops 270531584 | bytes 4984832 | tf_op jit(solution)/shard_map/qhd,khd->hqk/dot_general | solution.py:40
  75.8 0.4 fusion.175
  76.1 1.8 reshape.409
  77.9 0.7 bitcast_convert_fusion
  78.6 1.3 multiply_reduce_fusion.6
  80.0 43.2 %all_gather.7 = bf16[1280,256]{1,0:T(8,128)(2,1)} all-gather(bf16[40,256]{1,0:T(8,128)(2,1)S(1)} %bitcast.165), channel_id=1, replica_groups=mesh['ctx'=32,'head'=8] {'ctx'}, dimensions={0}, use_global_device_ids=true | all-gather | bytes 675840 | tf_op jit(solution)/shard_map/all_gather | solution.py:89
  123.2 1.9 fusion.167
  125.1 1.9 copy.152
  126.9 1.9 slice.85
  128.8 2.0 %copy.279 = bf16[1024,256]{0,1:T(8,128)(2,1)} copy(bf16[1024,256]{1,0:T(8,128)(2,1)} %slice.85) | data formatting | bytes 1048576
  130.9 0.8 copy.281
  131.6 0.7 multiply_reduce_fusion.5
  132.6 1.5 collective-permute-start.9
  134.1 1.4 fusion.169
  135.5 1.6 multiply_reduce_fusion
  137.4 1.4 fusion.170
  138.7 1.6 multiply_reduce_fusion.1
  140.4 2.9 %collective-permute-start.5 = (bf16[640,256]{0,1:T(8,128)(2,1)S(1)}, bf16[640,256]{0,1:T(8,128)(2,1)S(1)}, u32[]{:S(2)}, u32[]{:S(2)}) collective-permute-start(bf16[640,256]{0,1:T(8,128)(2,1)S(1)} %copy-done.8), channel_id=1, source_target_pairs={{0,32},{8,40},{16,48},{24,56},{32,0},{40,8},{48,16},{56,24},{64,96... | collective-permute-start | bytes 983048 | tf_op jit(solution)/shard_map/ppermute | solution.py:13
  143.3 1.4 fusion.171
  144.7 1.6 multiply_reduce_fusion.2
  146.3 1.2 collective-permute-start.3
  147.5 1.4 fusion.172
  148.8 1.6 multiply_reduce_fusion.3
  150.6 1.6 multiply_reduce_fusion.4
  152.2 1.4 fusion.174
  153.6 1.3 fusion.3
  155.0 1.3 fusion.9
  156.3 9.2 %collective-permute-done.7 = bf16[640,256]{0,1:T(8,128)(2,1)S(1)} collective-permute-done((bf16[640,256]{0,1:T(8,128)(2,1)S(1)}, bf16[640,256]{0,1:T(8,128)(2,1)S(1)}, u32[]{:S(2)}, u32[]{:S(2)}) %collective-permute-start.7) | collective-permute-done | bytes 327712 | tf_op jit(solution)/shard_map/ppermute | solution.py:13
  165.5 0.3 fusion.129
  165.8 0.7 fusion.23
  166.6 0.3 fusion.131
  166.9 0.4 fusion.115
  167.2 0.7 fusion.25
  168.0 0.7 fusion.21
  168.9 0.4 fusion.123
  169.2 0.3 fusion.127
  169.5 0.4 fusion.109
  170.1 0.4 fusion.121
  170.4 1.0 copy-done
  171.5 1.1 fusion.15
  172.9 0.7 fusion.1
  173.6 0.7 fusion.27
  174.3 1.3 fusion.5
  175.7 0.3 fusion.133
  176.0 0.4 fusion.111
  176.4 0.5 fusion.93
  177.0 0.9 fusion.48
  177.9 1.5 fusion.87
  179.4 0.4 fusion.103
  180.0 0.3 copy.213
  180.6 13.9 %all_to_all.19 = bf16[8,80,256]{2,1,0:T(8,128)(2,1)S(1)} all-to-all(bf16[8,80,256]{2,1,0:T(8,128)(2,1)S(1)} %all_to_all.14), channel_id=1, replica_groups=mesh['ctx'=32,'head'=8] {'head'}, dimensions={0} | all-to-all | bytes 655360 | tf_op jit(solution)/shard_map/all_to_all | solution.py:94
  194.5 0.8 copy.289
  (58 shorter events, 2.6 us)
Async XLA Ops:
  0.0 71.1 %slice-start.2 = ((bf16[640,256]{1,0:T(8,128)(2,1)}), bf16[512,256]{1,0:T(8,128)(2,1)S(1)}, s32[]{:S(2)}) async-start(bf16[640,256]{1,0:T(8,128)(2,1)} %param.5), calls=%async_computation.3 | async-start | bytes 524288 | tf_op jit(solution)/shard_map/slice | solution.py:42
  1.9 69.6 %slice-start.3 = ((bf16[640,256]{1,0:T(8,128)(2,1)}), bf16[128,256]{1,0:T(8,128)(2,1)S(1)}, s32[]{:S(2)}) async-start(bf16[640,256]{1,0:T(8,128)(2,1)} %param.5), calls=%async_computation.4 | async-start | bytes 131072 | tf_op jit(solution)/shard_map/slice | solution.py:42
  1.9 69.7 %copy-start.1 = (bf16[640,256]{1,0:T(8,128)(2,1)S(1)}, bf16[640,256]{1,0:T(8,128)(2,1)}, u32[]{:S(2)}) copy-start(bf16[640,256]{1,0:T(8,128)(2,1)} %param.6) | copy-start | bytes 983044
  1.9 130.4 %collective-permute-start.8 = (bf16[640,256]{0,1:T(8,128)(2,1)}, bf16[640,256]{0,1:T(8,128)(2,1)}, u32[]{:S(2)}, u32[]{:S(2)}) collective-permute-start(bf16[640,256]{0,1:T(8,128)(2,1)} %copy.149), channel_id=1, source_target_pairs={{0,128},{8,136},{16,144},{24,152},{32,160},{40,168},{48,176},{56,1... | collective-permute-start | bytes 983048 | tf_op jit(solution)/shard_map/ppermute | solution.py:13
  9.1 128.0 %collective-permute-start.6 = (bf16[640,256]{0,1:T(8,128)(2,1)}, bf16[640,256]{0,1:T(8,128)(2,1)}, u32[]{:S(2)}, u32[]{:S(2)}) collective-permute-start(bf16[640,256]{0,1:T(8,128)(2,1)} %copy.149), channel_id=1, source_target_pairs={{0,64},{8,72},{16,80},{24,88},{32,96},{40,104},{48,112},{56,120},{... | collective-permute-start | bytes 983048 | tf_op jit(solution)/shard_map/ppermute | solution.py:13
  10.6 129.8 %collective-permute-start.4 = (bf16[640,256]{0,1:T(8,128)(2,1)}, bf16[640,256]{0,1:T(8,128)(2,1)}, u32[]{:S(2)}, u32[]{:S(2)}) collective-permute-start(bf16[640,256]{0,1:T(8,128)(2,1)} %copy.149), channel_id=1, source_target_pairs={{0,32},{8,40},{16,48},{24,56},{32,0},{40,8},{48,16},{56,24},{64,96... | collective-permute-start | bytes 983048 | tf_op jit(solution)/shard_map/ppermute | solution.py:13
  11.6 134.7 %collective-permute-start.2 = (bf16[640,256]{0,1:T(8,128)(2,1)}, bf16[640,256]{0,1:T(8,128)(2,1)}, u32[]{:S(2)}, u32[]{:S(2)}) collective-permute-start(bf16[640,256]{0,1:T(8,128)(2,1)} %copy.149), channel_id=1, source_target_pairs={{0,16},{8,24},{16,0},{24,8},{32,48},{40,56},{48,32},{56,40},{64,80... | collective-permute-start | bytes 983048 | tf_op jit(solution)/shard_map/ppermute | solution.py:13
  11.9 138.5 %collective-permute-start = (bf16[640,256]{0,1:T(8,128)(2,1)}, bf16[640,256]{0,1:T(8,128)(2,1)}, u32[]{:S(2)}, u32[]{:S(2)}) collective-permute-start(bf16[640,256]{0,1:T(8,128)(2,1)} %copy.149), channel_id=1, source_target_pairs={{0,8},{8,0},{16,24},{24,16},{32,40},{40,32},{48,56},{56,48},{64,72... | collective-permute-start | bytes 983048 | tf_op jit(solution)/shard_map/ppermute | solution.py:13
  70.3 0.8 copy-start.4
  73.0 2.7 %slice-start.1 = ((bf16[1280,256]{1,0:T(8,128)(2,1)}), bf16[256,256]{1,0:T(8,128)(2,1)S(1)}, s32[]{:S(2)}) async-start(bf16[1280,256]{1,0:T(8,128)(2,1)} %copy-done.4), calls=%async_computation.2 | async-start | bytes 262144 | tf_op jit(solution)/shard_map/slice | solution.py:43
  75.7 4.2 %copy-start.6 = (bf16[256,256]{0,1:T(8,128)(2,1)}, bf16[256,256]{0,1:T(8,128)(2,1)S(1)}, u32[]{:S(2)}) copy-start(bf16[256,256]{0,1:T(8,128)(2,1)S(1)} %copy.280) | copy-start | bytes 393220
  123.2 7.7 %slice-start = ((bf16[1280,256]{1,0:T(8,128)(2,1)}), bf16[256,256]{1,0:T(8,128)(2,1)S(1)}, s32[]{:S(2)}) async-start(bf16[1280,256]{1,0:T(8,128)(2,1)} %all_gather.7), calls=%async_computation.1 | async-start | bytes 262144 | tf_op jit(solution)/shard_map/slice | solution.py:55
  131.6 1.0 copy-start.8
  132.6 35.3 %collective-permute-start.9 = (bf16[640,256]{0,1:T(8,128)(2,1)S(1)}, bf16[640,256]{0,1:T(8,128)(2,1)S(1)}, u32[]{:S(2)}, u32[]{:S(2)}) collective-permute-start(bf16[640,256]{0,1:T(8,128)(2,1)S(1)} %copy-done.8), channel_id=1, source_target_pairs={{0,128},{8,136},{16,144},{24,152},{32,160},{40,168},{48,176},{56,1... | collective-permute-start | bytes 983048 | tf_op jit(solution)/shard_map/ppermute | solution.py:13
  137.1 28.4 %collective-permute-start.7 = (bf16[640,256]{0,1:T(8,128)(2,1)S(1)}, bf16[640,256]{0,1:T(8,128)(2,1)S(1)}, u32[]{:S(2)}, u32[]{:S(2)}) collective-permute-start(bf16[640,256]{0,1:T(8,128)(2,1)S(1)} %copy-done.8), channel_id=1, source_target_pairs={{0,64},{8,72},{16,80},{24,88},{32,96},{40,104},{48,112},{56,120},{... | collective-permute-start | bytes 983048 | tf_op jit(solution)/shard_map/ppermute | solution.py:13
  140.4 26.2 %collective-permute-start.5 = (bf16[640,256]{0,1:T(8,128)(2,1)S(1)}, bf16[640,256]{0,1:T(8,128)(2,1)S(1)}, u32[]{:S(2)}, u32[]{:S(2)}) collective-permute-start(bf16[640,256]{0,1:T(8,128)(2,1)S(1)} %copy-done.8), channel_id=1, source_target_pairs={{0,32},{8,40},{16,48},{24,56},{32,0},{40,8},{48,16},{56,24},{64,96... | collective-permute-start | bytes 983048 | tf_op jit(solution)/shard_map/ppermute | solution.py:13
  146.3 27.3 %collective-permute-start.3 = (bf16[640,256]{0,1:T(8,128)(2,1)S(1)}, bf16[640,256]{0,1:T(8,128)(2,1)S(1)}, u32[]{:S(2)}, u32[]{:S(2)}) collective-permute-start(bf16[640,256]{0,1:T(8,128)(2,1)S(1)} %copy-done.8), channel_id=1, source_target_pairs={{0,16},{8,24},{16,0},{24,8},{32,48},{40,56},{48,32},{56,40},{64,80... | collective-permute-start | bytes 983048 | tf_op jit(solution)/shard_map/ppermute | solution.py:13
  150.5 27.4 %collective-permute-start.1 = (bf16[640,256]{0,1:T(8,128)(2,1)S(1)}, bf16[640,256]{0,1:T(8,128)(2,1)S(1)}, u32[]{:S(2)}, u32[]{:S(2)}) collective-permute-start(bf16[640,256]{0,1:T(8,128)(2,1)S(1)} %copy-done.8), channel_id=1, source_target_pairs={{0,8},{8,0},{16,24},{24,16},{32,40},{40,32},{48,56},{56,48},{64,72... | collective-permute-start | bytes 983048 | tf_op jit(solution)/shard_map/ppermute | solution.py:13
  153.6 1.4 copy-start.9
  167.9 0.9 copy-start.7
  168.8 1.2 copy-start.2
  169.2 2.2 %copy-start = (f32[2,1024,512]{2,1,0:T(8,128)S(1)}, f32[2,1024,512]{2,1,0:T(8,128)}, u32[]{:S(2)}) copy-start(f32[2,1024,512]{2,1,0:T(8,128)} %get-tuple-element.56) | copy-start | bytes 12582916
  171.5 1.2 copy-start.5
  174.3 2.1 %copy-start.3 = (bf16[640,256]{1,0:T(8,128)(2,1)S(1)}, bf16[640,256]{1,0:T(8,128)(2,1)}, u32[]{:S(2)}) copy-start(bf16[640,256]{1,0:T(8,128)(2,1)} %param.7) | copy-start | bytes 983044
where the time goes:
time: 196 us; the launch traced here: 195 us
  blocking collectives  113 us (58%)
  matrix products  31.2 us (16%)
  starting transfers between devices  16 us (8%)
  local copies, waits for them, and re-layouts  15.4 us (8%)
  other arithmetic  9.62 us (5%)
  waiting for transfers between devices  9.24 us (5%)
    all_gather x1, blocking collectives, body(): lax.all_gather(folded_keys, 'ctx', axis=0, tiled=True)  56.2 us
    all_gather x1, blocking collectives, body(): lax.all_gather(folded_values, 'ctx', axis=0, tiled=True)  43.2 us
    dot_general x16, matrix products, attend(): jnp.einsum('qhd,khd->hqk', query_heads[query_start:query_end], key_heads[...  21.8 us
    ppermute x10, starting transfers between devices, from_partner(): lax.ppermute(shard, axis, [(i, i ^ 1 << stride) for i in range(lax.axis_s...  16 us
    all_to_all x1, blocking collectives, body(): lax.all_to_all(result, 'head', split_axis=0, concat_axis=1, tiled=True)  13.9 us
    dot_general x16, matrix products, attend(): jnp.einsum('hqk,khd->hqd', weights.astype(jnp.bfloat16), value_heads[key_...  9.46 us
    unnamed x32, local copies, waits for them, and re-layouts  9.32 us
    ppermute x10, waiting for transfers between devices, from_partner(): lax.ppermute(shard, axis, [(i, i ^ 1 << stride) for i in range(lax.axis_s...  9.24 us
  transfers between devices with their start and end apart: 10, of which 1 were waited for; matrix products, arithmetic and copies ran while one was open for 25% of the time, Pallas kernels for 0%

commit v1 on v0

v1 whole, which is shorter than its diff:
```python
import functools
import math

import jax
import jax.numpy as jnp
from jax import lax
from jax.experimental import pallas as pl
from jax.experimental.pallas import tpu as pltpu
from jax.sharding import PartitionSpec as P


vmem_spec = pl.BlockSpec(memory_space=pltpu.VMEM)


def z_perm(size, target):
    return [(i, target(i // 4) % (size // 4) * 4 + i % 4) for i in range(size)]


def bit_perm(size, bit):
    return [(i, i ^ (1 << bit)) for i in range(size)]


def fold_kernel(keys, values, key_weight, value_weight, folded):
    for side, (rows, weight) in enumerate(((keys, key_weight), (values, value_weight))):
        head_count, group, width = weight.shape
        for head in range(head_count):
            lanes = slice(head * width, (head + 1) * width)
            block = rows[:, lanes].astype(jnp.float32)
            grouped = block.reshape(block.shape[0] // group, group, width)
            summed = jnp.sum(grouped * weight[head].astype(jnp.float32)[None], axis=1)
            folded[side, :, lanes] = summed.astype(folded.dtype)


def fold_rows(keys, values, key_weight, value_weight):
    rows, channels = keys.shape
    group = key_weight.shape[1]
    return pl.pallas_call(
        fold_kernel,
        name="fold_rows",
        out_shape=jax.ShapeDtypeStruct((2, rows // group, channels), keys.dtype),
        in_specs=[vmem_spec] * 4,
        out_specs=vmem_spec,
        compiler_params=pltpu.CompilerParams(vmem_limit_bytes=16 << 20),
        cost_estimate=pl.CostEstimate(flops=4 * rows * channels, bytes_accessed=4 * rows * channels, transcendentals=0),
    )(keys, values, key_weight, value_weight)


def attend_kernel(pieces, first, last, width, *refs):
    queries, rest = refs[0], refs[1:]
    keys, values, rest = rest[:pieces], rest[pieces : 2 * pieces], rest[2 * pieces :]
    if not first:
        top_in, total_in, sum_in, rest = *rest[:3], rest[3:]
    heads = queries.shape[1] // width
    factor = math.log2(math.e) / math.sqrt(width)

    for head in range(heads):
        lanes = slice(head * width, (head + 1) * width)
        query = queries[:, lanes]
        scores = [
            lax.dot_general(query, k[:, lanes], (((1,), (1,)), ((), ())), preferred_element_type=jnp.float32)
            for k in keys
        ]
        top = functools.reduce(jnp.maximum, [jnp.max(s, axis=1, keepdims=True) for s in scores])
        if not first:
            top_before = top_in[:, lanes][:, :1]
            top = jnp.maximum(top, top_before)
        weights = [jnp.exp2((s - top) * factor) for s in scores]
        total = sum(jnp.sum(w, axis=1, keepdims=True) for w in weights)
        summed = sum(
            jnp.dot(w.astype(jnp.bfloat16), v[:, lanes], preferred_element_type=jnp.float32)
            for w, v in zip(weights, values)
        )
        if not first:
            decay = jnp.exp2((top_before - top) * factor)
            total = total + decay * total_in[:, lanes][:, :1]
            summed = summed + decay * sum_in[:, lanes]
        if last:
            rest[0][:, lanes] = (summed * (1.0 / total)).astype(jnp.bfloat16)
        else:
            rest[0][:, lanes] = jnp.broadcast_to(top, summed.shape)
            rest[1][:, lanes] = jnp.broadcast_to(total, summed.shape)
            rest[2][:, lanes] = summed


def attend(carried, queries, pairs, width, last=False):
    rows, channels = queries.shape
    keys, values = [k for k, _ in pairs], [v for _, v in pairs]
    key_count = sum(k.shape[0] for k in keys)
    operands = [queries, *keys, *values, *(carried or ())]
    if last:
        out_shape = jax.ShapeDtypeStruct((rows, channels), jnp.bfloat16)
        out_specs = vmem_spec
    else:
        out_shape = [jax.ShapeDtypeStruct((rows, channels), jnp.float32)] * 3
        out_specs = [vmem_spec] * 3
    return pl.pallas_call(
        functools.partial(attend_kernel, len(pairs), carried is None, last, width),
        name="attend",
        out_shape=out_shape,
        in_specs=[vmem_spec] * len(operands),
        out_specs=out_specs,
        compiler_params=pltpu.CompilerParams(vmem_limit_bytes=16 << 20),
        cost_estimate=pl.CostEstimate(
            flops=8 * rows * key_count * channels,
            bytes_accessed=4 * key_count * channels + 4 * rows * channels,
            transcendentals=rows * key_count * channels // width,
        ),
    )(*operands)


def move(rows, pairs):
    return lax.ppermute(rows, "ctx", pairs)


def body(queries, keys, values, key_weight, value_weight):
    width = key_weight.shape[2]
    size = lax.axis_size("ctx")
    core, y_side, z_one, z_two, z_four = (bit_perm(size, bit) for bit in range(5))
    z_side = z_perm(size, lambda z: z + 2 if z & 2 else z - 2)
    z_odd = z_perm(size, lambda z: z + 1 if z & 1 else z - 1)

    folded = fold_rows(keys, values, key_weight, value_weight)
    for pairs in (z_four, z_side, z_odd, y_side, core):
        folded = jnp.concatenate([folded, move(folded, pairs)], 1)
    two = move(keys, z_two), move(values, z_two)
    one = move(keys, z_one), move(values, z_one)
    twin = move(keys, core), move(values, core)
    side = move(keys, y_side), move(values, y_side)
    four = move(two[0], z_side), move(two[1], z_side)

    stages = (
        ("own", ((keys, values), twin)),
        ("side", (side,)),
        ("two", (two,)),
        ("one", (one,)),
        ("comp", ((folded[0], folded[1]),)),
        ("four", (four,)),
    )
    carried = None
    for name, pairs in stages:
        carried = attend(carried, queries, pairs, width, last=name == "four")
    return lax.all_to_all(carried, "head", split_axis=0, concat_axis=1, tiled=True)


def solution(mesh):
    in_specs = (
        P("ctx", "head"),
        P("ctx", "head"),
        P("ctx", "head"),
        P("head", None, None),
        P("head", None, None),
    )
    out_specs = P(("ctx", "head"), None)

    return jax.shard_map(body, mesh=mesh, in_specs=in_specs, out_specs=out_specs, check_vma=False)
```

time: 196 us -> 120 us (0.61)
  blocking collectives: 113 us -> 12.8 us
  waiting for transfers between devices: 9.24 us -> 59.3 us
  matrix products: 31.2 us -> 0 us
  Pallas kernels: 0 us -> 17.1 us
  local copies, waits for them, and re-layouts: 15.4 us -> 3.34 us
  starting transfers between devices: 16 us -> 25.9 us
  other arithmetic: 9.62 us -> 0.04 us
    all_gather x2 -> x0, blocking collectives: 99.4 us -> none  [the longest x1 56.2 us: body(): lax.all_gather(folded_keys, 'ctx', axis=0, tiled=True)]
    ppermute x10 -> x15, waiting for transfers between devices: 9.24 us -> 59.3 us  [move(): return lax.ppermute(rows, 'ctx', pairs)]
    dot_general x32 -> x0, matrix products: 31.2 us -> none  [the longest x16 21.8 us: attend(): jnp.einsum('qhd,khd->hqk', query_heads[query_start:query_end], key_heads[...]
    pallas_call x0 -> x7, Pallas kernels: none -> 17.1 us  [the longest x6 15.9 us: attend(): pl.pallas_call(functools.partial(attend_kernel, len(pairs), carried is No...]
    ppermute x10 -> x15, starting transfers between devices: 16 us -> 25.9 us  [move(): return lax.ppermute(rows, 'ctx', pairs)]
    unnamed x32 -> x12, local copies, waits for them, and re-layouts: 9.32 us -> 2.42 us
    reduce_sum x10 -> x0, other arithmetic: 6.17 us -> none  [attend(): run_total = run_total * factor + jnp.sum(weights, axis=2)]
    reshape x2 -> x0, local copies, waits for them, and re-layouts: 2.83 us -> none  [fold_rows(): values_in.reshape(row_count // group_size, group_size, head_count, head_w...]
  transfers between devices with their start and end apart: 10 -> 15, of which waited for: 1 -> 6; matrix products, arithmetic and copies ran while one was open for 25% -> 0% of each run, Pallas kernels for 0% -> 12%
where the time goes in v1:
time: 120 us; the launch traced here: 119 us
  waiting for transfers between devices  59.3 us (49%)
  starting transfers between devices  25.9 us (22%)
  Pallas kernels  17.1 us (14%)
  blocking collectives  12.8 us (11%)
  local copies, waits for them, and re-layouts  3.34 us (3%)
    ppermute x15, waiting for transfers between devices, move(): return lax.ppermute(rows, 'ctx', pairs)  59.3 us
    ppermute x15, starting transfers between devices, move(): return lax.ppermute(rows, 'ctx', pairs)  25.9 us
    pallas_call x6, Pallas kernels, attend(): pl.pallas_call(functools.partial(attend_kernel, len(pairs), carried is No...  15.9 us
    all_to_all x1, blocking collectives, body(): lax.all_to_all(carried, 'head', split_axis=0, concat_axis=1, tiled=True)  12.8 us
    unnamed x12, local copies, waits for them, and re-layouts  2.42 us
  transfers between devices with their start and end apart: 15, of which 6 were waited for; matrix products, arithmetic and copies ran while one was open for 0% of the time, Pallas kernels for 12%

profile of v1, /device:TPU:16, one launch (start us, length us, event | category | flops | bytes accessed | tf_op | source)
XLA Modules:
  0.0 118.7 jit_solution(9143088290000746698)
XLA Ops:
  0.0 0.0 copy-start.1
  0.0 1.0 copy-done.1
  1.0 0.0 copy-start.2
  1.0 0.7 copy-done.2
  1.7 0.0 copy-start.3
  1.7 0.7 copy-done.3
  2.4 1.3 %fold_rows.1 = bf16[2,40,256]{2,1,0:T(8,128)(2,1)S(1)} custom-call(bf16[640,256]{1,0:T(8,128)(2,1)S(1)} %copy-done.1, bf16[640,256]{1,0:T(8,128)(2,1)} %refs_3_.1, bf16[2,16,128]{2,1,0:T(8,128)(2,1)S(1)} %copy-done.2, bf16[2,16,128]{2,1,0:T(8,128)(2,1)S(1)} %copy-done.3), custom_call_target="tpu_custom_call" | custom-call | flops 655360 | bytes 655360 | tf_op jit(solution)/shard_map/fold_rows/pallas_call | solution.py:37
  3.6 7.3 %collective-permute-start.4 = (bf16[2,40,256]{2,1,0:T(8,128)(2,1)S(1)}, bf16[2,40,256]{2,1,0:T(8,128)(2,1)S(1)}, u32[]{:S(2)}, u32[]{:S(2)}) collective-permute-start(bf16[2,40,256]{2,1,0:T(8,128)(2,1)S(1)} %fold_rows.1), channel_id=1, source_target_pairs={{0,128},{8,136},{16,144},{24,152},{32,160},{40,168},{48,176},{56,1... | collective-permute-start | bytes 122888 | tf_op jit(solution)/shard_map/ppermute | solution.py:112
  10.9 2.1 %collective-permute-done.4 = bf16[2,40,256]{2,1,0:T(8,128)(2,1)S(1)} collective-permute-done((bf16[2,40,256]{2,1,0:T(8,128)(2,1)S(1)}, bf16[2,40,256]{2,1,0:T(8,128)(2,1)S(1)}, u32[]{:S(2)}, u32[]{:S(2)}) %collective-permute-start.4) | collective-permute-done | bytes 40992 | tf_op jit(solution)/shard_map/ppermute | solution.py:112
  13.0 5.2 %collective-permute-start.5 = (bf16[2,80,256]{2,1,0:T(8,128)(2,1)S(1)}, bf16[2,80,256]{2,1,0:T(8,128)(2,1)S(1)}, u32[]{:S(2)}, u32[]{:S(2)}) collective-permute-start(bf16[2,80,256]{2,1,0:T(8,128)(2,1)S(1)} %pad_maximum_fusion.2), channel_id=1, source_target_pairs={{0,192},{8,200},{16,208},{24,216},{32,224},{40,232},{48,240},{56,2... | collective-permute-start | bytes 245768 | tf_op jit(solution)/shard_map/ppermute | solution.py:112
  18.2 2.9 %collective-permute-done.5 = bf16[2,80,256]{2,1,0:T(8,128)(2,1)S(1)} collective-permute-done((bf16[2,80,256]{2,1,0:T(8,128)(2,1)S(1)}, bf16[2,80,256]{2,1,0:T(8,128)(2,1)S(1)}, u32[]{:S(2)}, u32[]{:S(2)}) %collective-permute-start.5) | collective-permute-done | bytes 81952 | tf_op jit(solution)/shard_map/ppermute | solution.py:112
  21.0 0.0 copy-start
  21.1 3.2 %collective-permute-start.6 = (bf16[2,160,256]{2,1,0:T(8,128)(2,1)S(1)}, bf16[2,160,256]{2,1,0:T(8,128)(2,1)S(1)}, u32[]{:S(2)}, u32[]{:S(2)}) collective-permute-start(bf16[2,160,256]{2,1,0:T(8,128)(2,1)S(1)} %pad_maximum_fusion.1), channel_id=1, source_target_pairs={{0,224},{8,232},{16,240},{24,248},{32,64},{40,72},{48,80},{56,88},... | collective-permute-start | bytes 491528 | tf_op jit(solution)/shard_map/ppermute | solution.py:112
  24.3 0.0 collective-permute-start.13
  24.3 0.5 collective-permute-start.14
  24.8 0.3 collective-permute-start.11
  25.1 3.2 %collective-permute-start.12 = (bf16[640,256]{1,0:T(8,128)(2,1)}, bf16[640,256]{1,0:T(8,128)(2,1)S(1)}, u32[]{:S(2)}, u32[]{:S(2)}) collective-permute-start(bf16[640,256]{1,0:T(8,128)(2,1)} %refs_3_.1), channel_id=1, source_target_pairs={{0,16},{8,24},{16,0},{24,8},{32,48},{40,56},{48,32},{56,40},{64,80... | collective-permute-start | bytes 983048 | tf_op jit(solution)/shard_map/ppermute | solution.py:112
  28.3 0.0 collective-permute-done.6
  28.4 0.4 collective-permute-start.7
  28.8 21.1 %collective-permute-done.7 = bf16[2,320,256]{2,1,0:T(8,128)(2,1)S(1)} collective-permute-done((bf16[2,320,256]{2,1,0:T(8,128)(2,1)S(1)}, bf16[2,320,256]{2,1,0:T(8,128)(2,1)S(1)}, u32[]{:S(2)}, u32[]{:S(2)}) %collective-permute-start.7) | collective-permute-done | bytes 327712 | tf_op jit(solution)/shard_map/ppermute | solution.py:112
  50.0 0.1 collective-permute-start.8
  50.1 0.0 collective-permute-done.13.refs_2_
  50.1 0.1 collective-permute-start
  50.2 0.0 collective-permute-done.14.refs_4_
  50.2 2.9 %collective-permute-start.2 = (bf16[640,256]{1,0:T(8,128)(2,1)}, bf16[640,256]{1,0:T(8,128)(2,1)S(1)}, u32[]{:S(2)}, u32[]{:S(2)}) collective-permute-start(bf16[640,256]{1,0:T(8,128)(2,1)} %refs_3_.1), channel_id=1, source_target_pairs={{0,64},{8,72},{16,80},{24,88},{32,96},{40,104},{48,112},{56,120},{... | collective-permute-start | bytes 983048 | tf_op jit(solution)/shard_map/ppermute | solution.py:112
  53.1 0.0 collective-permute-done.11.refs_1_
  53.1 0.0 collective-permute-start.10
  53.1 0.0 collective-permute-done.12.refs_2_
  53.1 2.0 %collective-permute-start.9 = (bf16[640,256]{1,0:T(8,128)(2,1)S(1)}, bf16[640,256]{1,0:T(8,128)(2,1)S(1)}, u32[]{:S(2)}, u32[]{:S(2)}) collective-permute-start(bf16[640,256]{1,0:T(8,128)(2,1)S(1)} %copy-done.1), channel_id=1, source_target_pairs={{0,32},{8,40},{16,48},{24,56},{32,0},{40,8},{48,16},{56,24},{64,96... | collective-permute-start | bytes 983048 | tf_op jit(solution)/shard_map/ppermute | solution.py:112
  55.2 0.0 copy-done
  55.2 3.4 %attend.6 = (f32[640,256]{1,0:T(8,128)S(1)}, f32[640,256]{1,0:T(8,128)S(1)}, f32[640,256]{1,0:T(8,128)S(1)}) custom-call(bf16[640,256]{1,0:T(8,128)(2,1)S(1)} %copy-done, bf16[640,256]{1,0:T(8,128)(2,1)S(1)} %copy-done.1, bf16[640,256]{1,0:T(8,128)(2,1)S(1)} %collective-permute-done.13.refs_2_, bf16[640,256]{1,0:T(8,128)(2,1)} %refs_3_.1, ...), custom_call_target="tpu_custom_call" | custom-call | flops 1677721600 | bytes 1966080 | tf_op jit(solution)/shard_map/attend/pallas_call | solution.py:96
  58.6 16.0 %collective-permute-done.refs_1_ = bf16[640,256]{1,0:T(8,128)(2,1)S(1)} collective-permute-done((bf16[640,256]{1,0:T(8,128)(2,1)S(1)}, bf16[640,256]{1,0:T(8,128)(2,1)S(1)}, u32[]{:S(2)}, u32[]{:S(2)}) %collective-permute-start) | collective-permute-done | bytes 327712 | tf_op jit(solution)/shard_map/ppermute | solution.py:112
  74.6 0.4 collective-permute-start.1
  74.9 6.6 %collective-permute-done.2.refs_2_ = bf16[640,256]{1,0:T(8,128)(2,1)S(1)} collective-permute-done((bf16[640,256]{1,0:T(8,128)(2,1)}, bf16[640,256]{1,0:T(8,128)(2,1)S(1)}, u32[]{:S(2)}, u32[]{:S(2)}) %collective-permute-start.2) | collective-permute-done | bytes 327712 | tf_op jit(solution)/shard_map/ppermute | solution.py:112
  81.5 0.2 collective-permute-start.3
  81.8 2.1 %attend.7 = (f32[640,256]{1,0:T(8,128)S(1)}, f32[640,256]{1,0:T(8,128)S(1)}, f32[640,256]{1,0:T(8,128)S(1)}) custom-call(bf16[640,256]{1,0:T(8,128)(2,1)S(1)} %copy-done, bf16[640,256]{1,0:T(8,128)(2,1)S(1)} %collective-permute-done.11.refs_1_, bf16[640,256]{1,0:T(8,128)(2,1)S(1)} %collective-permute-done.12.refs_2_, ...), custom_call_target="tpu_custom_call" | custom-call | flops 838860800 | bytes 1310720 | tf_op jit(solution)/shard_map/attend/pallas_call | solution.py:96
  83.8 2.0 %attend.8 = (f32[640,256]{1,0:T(8,128)S(1)}, f32[640,256]{1,0:T(8,128)S(1)}, f32[640,256]{1,0:T(8,128)S(1)}) custom-call(bf16[640,256]{1,0:T(8,128)(2,1)S(1)} %copy-done, bf16[640,256]{1,0:T(8,128)(2,1)S(1)} %collective-permute-done.refs_1_, bf16[640,256]{1,0:T(8,128)(2,1)S(1)} %collective-permute-done.2.refs_2_, f32[640,256]{1,0:T(8,128)S(1)} %get-tuple-element.23.refs_3_, ...), custom_call_target="tpu_custom_call" | custom-call | flops 838860800 | bytes 1310720 | tf_op jit(solution)/shard_map/attend/pallas_call | solution.py:96
  85.9 0.0 collective-permute-done.10.refs_2_
  85.9 0.0 collective-permute-done.9.refs_1_
  85.9 2.1 %attend.9 = (f32[640,256]{1,0:T(8,128)S(1)}, f32[640,256]{1,0:T(8,128)S(1)}, f32[640,256]{1,0:T(8,128)S(1)}) custom-call(bf16[640,256]{1,0:T(8,128)(2,1)S(1)} %copy-done, bf16[640,256]{1,0:T(8,128)(2,1)S(1)} %collective-permute-done.9.refs_1_, bf16[640,256]{1,0:T(8,128)(2,1)S(1)} %collective-permute-done.10.refs_2_, ...), custom_call_target="tpu_custom_call" | custom-call | flops 838860800 | bytes 1310720 | tf_op jit(solution)/shard_map/attend/pallas_call | solution.py:96
  88.0 0.0 collective-permute-done.8
  88.0 0.1 slice_bitcast_fusion
  88.1 4.2 %attend.10 = (f32[640,256]{1,0:T(8,128)S(1)}, f32[640,256]{1,0:T(8,128)S(1)}, f32[640,256]{1,0:T(8,128)S(1)}) custom-call(bf16[640,256]{1,0:T(8,128)(2,1)S(1)} %copy-done, bf16[1280,256]{1,0:T(8,128)(2,1)S(1)} %get-tuple-element.36.refs_1_, bf16[1280,256]{1,0:T(8,128)(2,1)S(1)} %get-tuple-element.35.refs_2_, f32[640,256]{1,0:T(8,128)S(1)} %get-tuple-element.29.refs_3_, ...), custom_call_target="tpu_custom_call" | custom-call | flops 1677721600 | bytes 1966080 | tf_op jit(solution)/shard_map/attend/pallas_call | solution.py:96
  92.4 0.0 collective-permute-done.1.refs_1_
  92.4 10.7 %collective-permute-done.3.refs_2_ = bf16[640,256]{1,0:T(8,128)(2,1)S(1)} collective-permute-done((bf16[640,256]{1,0:T(8,128)(2,1)S(1)}, bf16[640,256]{1,0:T(8,128)(2,1)S(1)}, u32[]{:S(2)}, u32[]{:S(2)}) %collective-permute-start.3) | collective-permute-done | bytes 327712 | tf_op jit(solution)/shard_map/ppermute | solution.py:112
  103.0 2.0 %attend.11 = bf16[640,256]{1,0:T(8,128)(2,1)S(1)} custom-call(bf16[640,256]{1,0:T(8,128)(2,1)S(1)} %copy-done, bf16[640,256]{1,0:T(8,128)(2,1)S(1)} %collective-permute-done.1.refs_1_, bf16[640,256]{1,0:T(8,128)(2,1)S(1)} %collective-permute-done.3.refs_2_, f32[640,256]{1,0:T(8,128)S(1)} %get-tuple-element.32.refs_3_, ...), custom_call_target="tpu_custom_call" | custom-call | flops 838860800 | bytes 1310720 | tf_op jit(solution)/shard_map/attend/pallas_call | solution.py:96
  105.1 12.8 %all_to_all.19 = bf16[8,80,256]{2,1,0:T(8,128)(2,1)S(1)} all-to-all(bf16[8,80,256]{2,1,0:T(8,128)(2,1)S(1)} %bitcast.8), channel_id=1, replica_groups=mesh['ctx'=32,'head'=8] {'head'}, dimensions={0} | all-to-all | bytes 655360 | tf_op jit(solution)/shard_map/all_to_all | solution.py:142
  117.9 0.8 copy.7
  (9 shorter events, 0.2 us)
Async XLA Ops:
  0.0 1.0 copy-start.1
  1.0 0.7 copy-start.2
  1.7 0.7 copy-start.3
  3.6 9.3 %collective-permute-start.4 = (bf16[2,40,256]{2,1,0:T(8,128)(2,1)S(1)}, bf16[2,40,256]{2,1,0:T(8,128)(2,1)S(1)}, u32[]{:S(2)}, u32[]{:S(2)}) collective-permute-start(bf16[2,40,256]{2,1,0:T(8,128)(2,1)S(1)} %fold_rows.1), channel_id=1, source_target_pairs={{0,128},{8,136},{16,144},{24,152},{32,160},{40,168},{48,176},{56,1... | collective-permute-start | bytes 122888 | tf_op jit(solution)/shard_map/ppermute | solution.py:112
  13.0 8.0 %collective-permute-start.5 = (bf16[2,80,256]{2,1,0:T(8,128)(2,1)S(1)}, bf16[2,80,256]{2,1,0:T(8,128)(2,1)S(1)}, u32[]{:S(2)}, u32[]{:S(2)}) collective-permute-start(bf16[2,80,256]{2,1,0:T(8,128)(2,1)S(1)} %pad_maximum_fusion.2), channel_id=1, source_target_pairs={{0,192},{8,200},{16,208},{24,216},{32,224},{40,232},{48,240},{56,2... | collective-permute-start | bytes 245768 | tf_op jit(solution)/shard_map/ppermute | solution.py:112
  21.0 34.1 %copy-start = (bf16[640,256]{1,0:T(8,128)(2,1)S(1)}, bf16[640,256]{1,0:T(8,128)(2,1)}, u32[]{:S(2)}) copy-start(bf16[640,256]{1,0:T(8,128)(2,1)} %refs_0_.11) | copy-start | bytes 983044
  21.1 7.3 %collective-permute-start.6 = (bf16[2,160,256]{2,1,0:T(8,128)(2,1)S(1)}, bf16[2,160,256]{2,1,0:T(8,128)(2,1)S(1)}, u32[]{:S(2)}, u32[]{:S(2)}) collective-permute-start(bf16[2,160,256]{2,1,0:T(8,128)(2,1)S(1)} %pad_maximum_fusion.1), channel_id=1, source_target_pairs={{0,224},{8,232},{16,240},{24,248},{32,64},{40,72},{48,80},{56,88},... | collective-permute-start | bytes 491528 | tf_op jit(solution)/shard_map/ppermute | solution.py:112
  24.3 25.8 %collective-permute-start.13 = (bf16[640,256]{1,0:T(8,128)(2,1)S(1)}, bf16[640,256]{1,0:T(8,128)(2,1)S(1)}, u32[]{:S(2)}, u32[]{:S(2)}) collective-permute-start(bf16[640,256]{1,0:T(8,128)(2,1)S(1)} %copy-done.1), channel_id=1, source_target_pairs={{0,8},{8,0},{16,24},{24,16},{32,40},{40,32},{48,56},{56,48},{64,72... | collective-permute-start | bytes 983048 | tf_op jit(solution)/shard_map/ppermute | solution.py:112
  24.3 25.9 %collective-permute-start.14 = (bf16[640,256]{1,0:T(8,128)(2,1)}, bf16[640,256]{1,0:T(8,128)(2,1)S(1)}, u32[]{:S(2)}, u32[]{:S(2)}) collective-permute-start(bf16[640,256]{1,0:T(8,128)(2,1)} %refs_3_.1), channel_id=1, source_target_pairs={{0,8},{8,0},{16,24},{24,16},{32,40},{40,32},{48,56},{56,48},{64,72... | collective-permute-start | bytes 983048 | tf_op jit(solution)/shard_map/ppermute | solution.py:112
  24.8 28.3 %collective-permute-start.11 = (bf16[640,256]{1,0:T(8,128)(2,1)S(1)}, bf16[640,256]{1,0:T(8,128)(2,1)S(1)}, u32[]{:S(2)}, u32[]{:S(2)}) collective-permute-start(bf16[640,256]{1,0:T(8,128)(2,1)S(1)} %copy-done.1), channel_id=1, source_target_pairs={{0,16},{8,24},{16,0},{24,8},{32,48},{40,56},{48,32},{56,40},{64,80... | collective-permute-start | bytes 983048 | tf_op jit(solution)/shard_map/ppermute | solution.py:112
  25.1 28.0 %collective-permute-start.12 = (bf16[640,256]{1,0:T(8,128)(2,1)}, bf16[640,256]{1,0:T(8,128)(2,1)S(1)}, u32[]{:S(2)}, u32[]{:S(2)}) collective-permute-start(bf16[640,256]{1,0:T(8,128)(2,1)} %refs_3_.1), channel_id=1, source_target_pairs={{0,16},{8,24},{16,0},{24,8},{32,48},{40,56},{48,32},{56,40},{64,80... | collective-permute-start | bytes 983048 | tf_op jit(solution)/shard_map/ppermute | solution.py:112
  28.4 21.6 %collective-permute-start.7 = (bf16[2,320,256]{2,1,0:T(8,128)(2,1)S(1)}, bf16[2,320,256]{2,1,0:T(8,128)(2,1)S(1)}, u32[]{:S(2)}, u32[]{:S(2)}) collective-permute-start(bf16[2,320,256]{2,1,0:T(8,128)(2,1)S(1)} %pad_maximum_fusion), channel_id=1, source_target_pairs={{0,16},{8,24},{16,0},{24,8},{32,48},{40,56},{48,32},{56,40},{64,80... | collective-permute-start | bytes 983048 | tf_op jit(solution)/shard_map/ppermute | solution.py:112
  50.0 38.0 %collective-permute-start.8 = (bf16[2,640,256]{2,1,0:T(8,128)(2,1)S(1)}, bf16[2,640,256]{2,1,0:T(8,128)(2,1)S(1)}, u32[]{:S(2)}, u32[]{:S(2)}) collective-permute-start(bf16[2,640,256]{2,1,0:T(8,128)(2,1)S(1)} %get-tuple-element.37), channel_id=1, source_target_pairs={{0,8},{8,0},{16,24},{24,16},{32,40},{40,32},{48,56},{56,48},{64,72... | collective-permute-start | bytes 1966088 | tf_op jit(solution)/shard_map/ppermute | solution.py:112
  50.1 24.5 %collective-permute-start = (bf16[640,256]{1,0:T(8,128)(2,1)S(1)}, bf16[640,256]{1,0:T(8,128)(2,1)S(1)}, u32[]{:S(2)}, u32[]{:S(2)}) collective-permute-start(bf16[640,256]{1,0:T(8,128)(2,1)S(1)} %copy-done.1), channel_id=1, source_target_pairs={{0,64},{8,72},{16,80},{24,88},{32,96},{40,104},{48,112},{56,120},{... | collective-permute-start | bytes 983048 | tf_op jit(solution)/shard_map/ppermute | solution.py:112
  50.2 31.3 %collective-permute-start.2 = (bf16[640,256]{1,0:T(8,128)(2,1)}, bf16[640,256]{1,0:T(8,128)(2,1)S(1)}, u32[]{:S(2)}, u32[]{:S(2)}) collective-permute-start(bf16[640,256]{1,0:T(8,128)(2,1)} %refs_3_.1), channel_id=1, source_target_pairs={{0,64},{8,72},{16,80},{24,88},{32,96},{40,104},{48,112},{56,120},{... | collective-permute-start | bytes 983048 | tf_op jit(solution)/shard_map/ppermute | solution.py:112
  53.1 32.8 %collective-permute-start.10 = (bf16[640,256]{1,0:T(8,128)(2,1)}, bf16[640,256]{1,0:T(8,128)(2,1)S(1)}, u32[]{:S(2)}, u32[]{:S(2)}) collective-permute-start(bf16[640,256]{1,0:T(8,128)(2,1)} %refs_3_.1), channel_id=1, source_target_pairs={{0,32},{8,40},{16,48},{24,56},{32,0},{40,8},{48,16},{56,24},{64,96... | collective-permute-start | bytes 983048 | tf_op jit(solution)/shard_map/ppermute | solution.py:112
  53.1 32.8 %collective-permute-start.9 = (bf16[640,256]{1,0:T(8,128)(2,1)S(1)}, bf16[640,256]{1,0:T(8,128)(2,1)S(1)}, u32[]{:S(2)}, u32[]{:S(2)}) collective-permute-start(bf16[640,256]{1,0:T(8,128)(2,1)S(1)} %copy-done.1), channel_id=1, source_target_pairs={{0,32},{8,40},{16,48},{24,56},{32,0},{40,8},{48,16},{56,24},{64,96... | collective-permute-start | bytes 983048 | tf_op jit(solution)/shard_map/ppermute | solution.py:112
  74.6 17.8 %collective-permute-start.1 = (bf16[640,256]{1,0:T(8,128)(2,1)S(1)}, bf16[640,256]{1,0:T(8,128)(2,1)S(1)}, u32[]{:S(2)}, u32[]{:S(2)}) collective-permute-start(bf16[640,256]{1,0:T(8,128)(2,1)S(1)} %collective-permute-done.refs_1_), channel_id=1, source_target_pairs={{0,192},{8,200},{16,208},{24,216},{32,224},{40,232},{48,240},{56,2... | collective-permute-start | bytes 983048 | tf_op jit(solution)/shard_map/ppermute | solution.py:112
  81.5 21.5 %collective-permute-start.3 = (bf16[640,256]{1,0:T(8,128)(2,1)S(1)}, bf16[640,256]{1,0:T(8,128)(2,1)S(1)}, u32[]{:S(2)}, u32[]{:S(2)}) collective-permute-start(bf16[640,256]{1,0:T(8,128)(2,1)S(1)} %collective-permute-done.2.refs_2_), channel_id=1, source_target_pairs={{0,192},{8,200},{16,208},{24,216},{32,224},{40,232},{48,240},{56,2... | collective-permute-start | bytes 983048 | tf_op jit(solution)/shard_map/ppermute | solution.py:112
